TPU v7x, 512 devices: a whole 4x8x8 slice. The times are simulated.
512 devices in a mesh: seq: 8 (over z), vocab: 64 (over y, x, core).
Axes of the slice: x: 4, y: 8, z: 8, core: 2. Of those that a mesh axis runs over, the one named last changes fastest.
Arguments:
- hidden: bfloat16 [2048, 8192], P('seq', 'vocab'), may hold values from -120 to 120
- head_weight: bfloat16 [8192, 98304], P('seq', 'vocab'), may hold values from -0.0625 to 0.0625
- vocab_basis: bfloat16 [98304, 1024], P('vocab', 'seq'), may hold values from -0.0048828125 to 0.0048828125
- keep_index: int32 [512], P('seq'), may hold values from 0 to 255, as said below
- counts: int32 [8], P('seq'), may hold values from 1 to 64, as said below
Outputs:
- coefficients: float32 [512, 1024], P('seq', 'vocab')
Inputs may be any that keep to these rules, and one draw needn't show every extreme that they name: `keep_index`: each owner's list is strictly increasing and ends at 255. `counts`: exactly one owner has all 64 slots live.
All inputs are finite; a program needn't handle non-finite values.
Results may differ from a plain program's by a relative error of at most 0.0032.
Values may be sent and summed in bfloat16 or wider, within the bound.
No kernel may reach another device: no remote copies, remote signals or barrier semaphores. Data moves between devices by JAX's collectives and lax.ppermute only.
A program may use at most 64 MiB of HBM per device.

v0:
```python
import jax
import jax.numpy as jnp
from jax import lax
from jax.sharding import PartitionSpec as P


def shards(hidden, head_weight, vocab_basis, keep_index, counts):
    chosen = jnp.take(hidden, keep_index, axis=0)
    features = lax.all_gather(chosen, "vocab", axis=1, tiled=True)
    pieces = lax.all_to_all(features, "seq", split_axis=1, concat_axis=0, tiled=True)
    owned = features.shape[0]
    logits = lax.psum_scatter(
        jnp.dot(pieces, head_weight, preferred_element_type=jnp.float32),
        "seq",
        scatter_dimension=0,
        tiled=True,
    )
    row_max = lax.pmax(jnp.max(logits, axis=1, keepdims=True), "vocab")
    weights = jnp.exp(logits - row_max)
    denominator, weighted = lax.psum(
        (jnp.sum(weights, axis=1, keepdims=True), jnp.sum(weights * logits, axis=1, keepdims=True)),
        "vocab",
    )
    expected = weighted / denominator
    centred = (logits - expected).astype(jnp.bfloat16)
    partial_sums = jnp.dot(
        centred,
        lax.all_gather(vocab_basis, "seq", axis=1, tiled=True),
        preferred_element_type=jnp.float32,
    )
    summed = lax.psum_scatter(partial_sums, "vocab", scatter_dimension=1, tiled=True)
    live_rows = jnp.arange(owned, dtype=jnp.int32) < counts[0]
    return jnp.where(live_rows[:, None], summed, jnp.float32(0.0))


def solution(mesh):
    in_specs = (P("seq", "vocab"), P("seq", "vocab"), P("vocab", "seq"), P("seq"), P("seq"))
    out_specs = P("seq", "vocab")
    return jax.shard_map(shards, mesh=mesh, in_specs=in_specs, out_specs=out_specs, check_vma=False)
```

profile of v0, /device:TPU:2, one launch (start us, length us, event | category | flops | bytes accessed | tf_op | source)
XLA Modules:
  0.0 629.6 jit_solution(8558448056872284931)
XLA Ops:
  6.5 0.0 copy-start
  6.5 0.0 all-gather.3.cloned.1.call-start
  6.5 0.8 compare_select_fusion
  7.3 0.8 compare_and_fusion
  8.2 1.5 gather_fusion
  9.6 0.7 broadcast_select_fusion
  10.3 0.0 all-gather.3.cloned.1.call-update
  10.3 0.0 reduce-scatter.2.cloned.1.call-start
  10.4 80.3 %all-gather.3.cloned.1.call-done = bf16[64,8192]{1,0:T(8,128)(2,1)} async-done(((bf16[64,128]{1,0:T(8,128)(2,1)}), bf16[64,8192]{1,0:T(8,128)(2,1)}) %all-gather.3.cloned.1.call-update) | async-done | bytes 1048592 | tf_op jit(solution)/shard_map/all_gather | solution.py:9
  90.7 1.3 copy.10
  92.0 36.3 %all_to_all.19 = bf16[64,8,1024]{2,0,1:T(8,128)(2,1)S(1)} all-to-all(bf16[64,8,1024]{2,0,1:T(8,128)(2,1)S(1)} %bitcast.17), channel_id=1, replica_groups=mesh['seq'=8,'vocab'=64] {'seq'}, dimensions={1} | all-to-all | bytes 2097152 | tf_op jit(solution)/shard_map/all_to_all | solution.py:10
  128.3 0.0 copy-done
  128.3 3.5 fusion.3
  131.8 0.0 reduce-scatter.2.cloned.1.call-update
  131.8 0.0 all-gather.5.cloned.1.call-start
  131.9 0.7 all-gather.5.cloned.1.call-update
  132.6 0.0 all-reduce.4.cloned.1.call-start
  132.6 43.5 %reduce-scatter.2.cloned.1.call-done = f32[64,1536]{1,0:T(8,128)} async-done(((f32[512,1536]{1,0:T(8,128)}), f32[64,1536]{1,0:T(8,128)}) %reduce-scatter.2.cloned.1.call-update) | async-done | bytes 393232 | tf_op jit(solution)/shard_map/reduce_scatter | solution.py:12
  176.1 1.1 reduce_max.9
  177.2 120.6 %pmax.7 = f32[64]{0:T(128)S(1)} all-reduce(f32[64]{0:T(128)S(1)} %reduce_max.9), channel_id=1, replica_groups=mesh['seq'=8,'vocab'=64] {'vocab'}, use_global_device_ids=true, to_apply=%region_2.3 | all-reduce | flops 64 | bytes 512 | tf_op jit(solution)/shard_map/pmax | solution.py:18
  297.8 1.2 fusion
  299.1 124.1 %all-reduce.1 = (f32[64,1]{0,1:T(1,128)S(1)}, f32[64,1]{0,1:T(1,128)S(1)}) all-reduce(f32[64,1]{0,1:T(1,128)S(1)} %bitcast.21, f32[64,1]{0,1:T(1,128)S(1)} %bitcast.20), channel_id=1, replica_groups=mesh['seq'=8,'vocab'=64] {'vocab'}, use_global_device_ids=true, to_apply=%region_4.5 | all-reduce | flops 128 | bytes 1024 | tf_op jit(solution)/shard_map/psum | solution.py:20
  423.1 0.0 all-gather.5.cloned.1.call-done
  423.2 4.2 fusion.1
  427.3 0.0 all-reduce.4.cloned.1.call-update
  428.0 1.3 dynamic-slice
  429.9 191.8 %all-reduce.4.cloned.1.call-done = f32[64,1024]{0,1:T(8,128)} async-done(((f32[64,1024]{0,1:T(8,128)}), f32[64,1024]{0,1:T(8,128)}) %all-reduce.4.cloned.1.call-update) | async-done | bytes 262160
  621.7 1.3 dynamic-slice_select_fusion
  (3 shorter events, 0.0 us)
Async XLA Ops:
  6.5 121.8 %copy-start = (bf16[1024,1536]{1,0:T(8,128)(2,1)S(1)}, bf16[1024,1536]{1,0:T(8,128)(2,1)}, u32[]{:S(2)}) copy-start(bf16[1024,1536]{1,0:T(8,128)(2,1)} %param.6) | copy-start | bytes 9437188
  6.5 84.1 %all-gather.3.cloned.1.call-start = ((), (), s32[]{:S(2)}) async-start(), calls=%async_computation.2 | async-start | bytes 1064960 | tf_op jit(solution)/shard_map/all_gather | solution.py:9
  10.3 165.7 %reduce-scatter.2.cloned.1.call-start = ((), (), s32[]{:S(2)}) async-start(), calls=%async_computation.3 | async-start | bytes 3538944 | tf_op jit(solution)/shard_map/reduce_scatter | solution.py:12
  131.8 291.3 %all-gather.5.cloned.1.call-start = ((), (), s32[]{:S(2)}) async-start(), calls=%async_computation.4 | async-start | bytes 3538944 | tf_op jit(solution)/shard_map/all_gather | solution.py:28
  132.6 489.2 %all-reduce.4.cloned.1.call-start = ((), (), s32[]{:S(2)}) async-start(), calls=%async_computation.5 | async-start | bytes 1048576
Sparse Core Ops, SparseCore 0:
  10.6 80.0 all-gather.2
  131.9 44.0 reduce-scatter.1
  178.1 57.3 all-gather.4
  427.5 194.2 all-reduce.3
where the time goes:
time: 630 us
  waiting for transfers between devices  316 us (50%)
  blocking collectives  281 us (45%)
  between operations  14.5 us (2%)
  matrix products  7.68 us (1%)
    unnamed x5, waiting for transfers between devices  193 us
    psum x1, blocking collectives, shards(): lax.psum((jnp.sum(weights, axis=1, keepdims=True), jnp.sum(weights * logi...  124 us
    pmax x1, blocking collectives, shards(): row_max = lax.pmax(jnp.max(logits, axis=1, keepdims=True), 'vocab')  121 us
    all_gather x1, waiting for transfers between devices, shards(): features = lax.all_gather(chosen, 'vocab', axis=1, tiled=True)  80.3 us
    reduce_scatter x1, waiting for transfers between devices, shards(): lax.psum_scatter(jnp.dot(pieces, head_weight, preferred_element_type=jnp....  43.5 us
    all_to_all x1, blocking collectives, shards(): lax.all_to_all(features, 'seq', split_axis=1, concat_axis=0, tiled=True)  36.3 us
  transfers between devices with their start and end apart: 4, of which 3 were waited for; matrix products, arithmetic and copies ran while one was open for 1% of the time, Pallas kernels for 0%

commit v1 on v0

--- a/solution.py
+++ b/solution.py
@@ -6,7 +6,10 @@
 
 def shards(hidden, head_weight, vocab_basis, keep_index, counts):
     chosen = jnp.take(hidden, keep_index, axis=0)
-    features = lax.all_gather(chosen, "vocab", axis=1, tiled=True)
+    size = lax.axis_size("vocab")
+    parts = jnp.stack([chosen for _ in range(size)])
+    parts = lax.all_to_all(parts, "vocab", split_axis=0, concat_axis=0)
+    features = jnp.concatenate(parts, axis=1)
     pieces = lax.all_to_all(features, "seq", split_axis=1, concat_axis=0, tiled=True)
     owned = features.shape[0]
     logits = lax.psum_scatter(

time: 630 us -> 593 us (0.941)
  waiting for transfers between devices: 316 us -> 235 us
  blocking collectives: 281 us -> 322 us
    all_gather x1 -> x0, waiting for transfers between devices: 80.3 us -> none  [shards(): features = lax.all_gather(chosen, 'vocab', axis=1, tiled=True)]
    all_to_all x0 -> x1, blocking collectives: none -> 39.2 us  [shards(): parts = lax.all_to_all(parts, 'vocab', split_axis=0, concat_axis=0)]
    unnamed x5 -> x4, waiting for transfers between devices: 193 us -> 193 us
  transfers between devices with their start and end apart: 4 -> 3, of which waited for: 3 -> 2; matrix products, arithmetic and copies ran while one was open for 1% -> 1% of each run, Pallas kernels for 0% -> 0%
where the time goes in v1:
time: 593 us; the launch traced here: 592 us
  blocking collectives  322 us (54%)
  waiting for transfers between devices  235 us (40%)
  between operations  14.4 us (2%)
  local copies, waits for them, and re-layouts  8.76 us (1%)
  matrix products  7.68 us (1%)
    unnamed x4, waiting for transfers between devices  193 us
    psum x1, blocking collectives, shards(): lax.psum((jnp.sum(weights, axis=1, keepdims=True), jnp.sum(weights * logi...  124 us
    pmax x1, blocking collectives, shards(): row_max = lax.pmax(jnp.max(logits, axis=1, keepdims=True), 'vocab')  120 us
    reduce_scatter x1, waiting for transfers between devices, shards(): lax.psum_scatter(jnp.dot(pieces, head_weight, preferred_element_type=jnp....  41.7 us
    all_to_all x1, blocking collectives, shards(): parts = lax.all_to_all(parts, 'vocab', split_axis=0, concat_axis=0)  39.2 us
    all_to_all x1, blocking collectives, shards(): lax.all_to_all(features, 'seq', split_axis=1, concat_axis=0, tiled=True)  37.9 us
  transfers between devices with their start and end apart: 3, of which 2 were waited for; matrix products, arithmetic and copies ran while one was open for 1% of the time, Pallas kernels for 0%

profile of v1, /device:TPU:2, one launch (start us, length us, event | category | flops | bytes accessed | tf_op | source)
XLA Modules:
  0.0 592.5 jit_solution(5772289169299730955)
XLA Ops:
  6.5 0.0 copy-start
  6.5 0.0 reduce-scatter.2.cloned.1.call-start
  6.5 0.8 compare_select_fusion
  7.3 0.8 compare_and_fusion
  8.2 1.5 gather_fusion
  9.6 0.1 broadcast_select_fusion
  9.7 0.2 stack.2
  10.0 39.2 %all_to_all.24 = bf16[64,64,128]{2,1,0:T(8,128)(2,1)S(1)} all-to-all(bf16[64,64,128]{2,1,0:T(8,128)(2,1)S(1)} %stack.2), channel_id=1, replica_groups=mesh['seq'=8,'vocab'=64] {'vocab'}, dimensions={0} | all-to-all | bytes 2097152 | tf_op jit(solution)/shard_map/all_to_all | solution.py:11
  49.2 1.7 copy.7
  50.8 2.3 all_to_all.18
  53.1 1.8 copy.8
  55.0 37.9 %all_to_all.25 = bf16[64,8,1024]{2,0,1:T(8,128)(2,1)S(1)} all-to-all(bf16[64,8,1024]{2,0,1:T(8,128)(2,1)S(1)} %copy.8), channel_id=1, replica_groups=mesh['seq'=8,'vocab'=64] {'seq'}, dimensions={1} | all-to-all | bytes 2097152 | tf_op jit(solution)/shard_map/all_to_all | solution.py:13
  92.8 0.0 copy-done
  92.8 3.5 fusion.3
  96.3 0.0 reduce-scatter.2.cloned.1.call-update
  96.4 0.0 all-gather.2.cloned.1.call-start
  96.4 0.7 all-gather.2.cloned.1.call-update
  97.1 0.0 all-reduce.4.cloned.1.call-start
  97.2 41.7 %reduce-scatter.2.cloned.1.call-done = f32[64,1536]{1,0:T(8,128)} async-done(((f32[512,1536]{1,0:T(8,128)}), f32[64,1536]{1,0:T(8,128)}) %reduce-scatter.2.cloned.1.call-update) | async-done | bytes 393232 | tf_op jit(solution)/shard_map/reduce_scatter | solution.py:15
  138.9 1.1 reduce_max.9
  140.0 120.4 %pmax.7 = f32[64]{0:T(128)S(1)} all-reduce(f32[64]{0:T(128)S(1)} %reduce_max.9), channel_id=1, replica_groups=mesh['seq'=8,'vocab'=64] {'vocab'}, use_global_device_ids=true, to_apply=%region_2.3 | all-reduce | flops 64 | bytes 512 | tf_op jit(solution)/shard_map/pmax | solution.py:21
  260.5 1.2 fusion
  261.7 124.1 %all-reduce.1 = (f32[64,1]{0,1:T(1,128)S(1)}, f32[64,1]{0,1:T(1,128)S(1)}) all-reduce(f32[64,1]{0,1:T(1,128)S(1)} %bitcast.17, f32[64,1]{0,1:T(1,128)S(1)} %bitcast.16), channel_id=1, replica_groups=mesh['seq'=8,'vocab'=64] {'vocab'}, use_global_device_ids=true, to_apply=%region_4.5 | all-reduce | flops 128 | bytes 1024 | tf_op jit(solution)/shard_map/psum | solution.py:23
  385.8 0.0 all-gather.2.cloned.1.call-done
  385.8 4.2 fusion.1
  390.0 0.0 all-reduce.4.cloned.1.call-update
  390.6 1.3 dynamic-slice
  392.6 192.1 %all-reduce.4.cloned.1.call-done = f32[64,1024]{0,1:T(8,128)} async-done(((f32[64,1024]{0,1:T(8,128)}), f32[64,1024]{0,1:T(8,128)}) %all-reduce.4.cloned.1.call-update) | async-done | bytes 262160
  584.6 1.3 dynamic-slice_select_fusion
  (3 shorter events, 0.0 us)
Async XLA Ops:
  6.5 86.3 %copy-start = (bf16[1024,1536]{1,0:T(8,128)(2,1)S(1)}, bf16[1024,1536]{1,0:T(8,128)(2,1)}, u32[]{:S(2)}) copy-start(bf16[1024,1536]{1,0:T(8,128)(2,1)} %param.6) | copy-start | bytes 9437188
  6.5 132.4 %reduce-scatter.2.cloned.1.call-start = ((), (), s32[]{:S(2)}) async-start(), calls=%async_computation.3 | async-start | bytes 3538944 | tf_op jit(solution)/shard_map/reduce_scatter | solution.py:15
  96.4 289.4 %all-gather.2.cloned.1.call-start = ((), (), s32[]{:S(2)}) async-start(), calls=%async_computation.4 | async-start | bytes 3538944 | tf_op jit(solution)/shard_map/all_gather | solution.py:31
  97.1 487.5 %all-reduce.4.cloned.1.call-start = ((), (), s32[]{:S(2)}) async-start(), calls=%async_computation.5 | async-start | bytes 1048576
Sparse Core Ops, SparseCore 0:
  96.5 42.3 reduce-scatter.1
  140.9 57.4 all-gather.1
  390.1 194.5 all-reduce.3
